TPU v7x, 512 devices: a whole 4x8x8 slice. The times are simulated.
512 devices in a mesh: ep: 64 (over z, x, core), tp: 8 (over y).
Axes of the slice: x: 4, y: 8, z: 8, core: 2. Of those that a mesh axis runs over, the one named last changes fastest.
Arguments:
- attn_out: bfloat16 [8192, 2048], P('ep', 'tp'), may hold values from -6 to 6
- resid: bfloat16 [8192, 2048], P(('ep', 'tp')), may hold values from -6 to 6
- norm_gain: float32 [2048], replicated, may hold values from 0.1 to 1.9
- expert_ids: int32 [8192, 6], P('ep'), may hold values from 0 to 63, all different within a row; in each aligned block of 128 rows (0 to 127, 128 to 255, ...) at most 16 rows name the same one
- gate_vals: float32 [8192, 6], P('ep'), may hold values from 0.1 to 1
- w_gate: bfloat16 [64, 1408, 2048], P('ep', 'tp'), may hold values from -0.125 to 0.125
- w_up: bfloat16 [64, 1408, 2048], P('ep', 'tp'), may hold values from -0.125 to 0.125
- w_down: bfloat16 [64, 1408, 2048], P('ep', 'tp'), may hold values from -0.15625 to 0.15625
Outputs:
- layer_out: bfloat16 [8192, 2048], P(('ep', 'tp'))
Inputs may be any that keep to these rules, and one draw needn't show every extreme that they name: `expert_ids`: among the tokens of one index of ep (aligned blocks of 128 rows), no expert is chosen by more than 16 tokens; some expert reaches 16 in some blocks. The experts of one token differ.
All inputs are finite; a program needn't handle non-finite values.
Results may differ from a plain program's by a relative error of at most 0.0095.
Values may be sent and summed in bfloat16 or wider, within the bound.
A program may use at most 64 MiB of HBM per device.

v0:
```python
import jax
import jax.numpy as jnp
from jax import lax
from jax.sharding import PartitionSpec as P

F32 = jnp.float32
BF16 = jnp.bfloat16


def per_device(attn_out, resid, norm_gain, expert_ids, gate_vals, w_gate, w_up, w_down):
    ep_count = lax.axis_size("ep")
    tok, top = expert_ids.shape
    cap = 4 * tok * top // (3 * ep_count)
    slots = ep_count * cap
    resid_cols = lax.all_to_all(resid, "tp", split_axis=1, concat_axis=0, tiled=True)
    down_cols = lax.all_to_all(w_down[0], "tp", split_axis=1, concat_axis=0, tiled=True)
    h = (resid_cols.astype(F32) + attn_out.astype(F32)).astype(BF16)
    hit = expert_ids[:, :, None] == jnp.arange(ep_count, dtype=jnp.int32)[None, None, :]
    chosen = jnp.any(hit, axis=1).astype(BF16)
    gates = jnp.sum(jnp.where(hit, gate_vals[:, :, None], 0.0), axis=1)
    earlier = jnp.tril(jnp.ones((tok, tok), BF16), -1)
    rank = jnp.dot(earlier, chosen, preferred_element_type=F32).astype(jnp.int32)
    place = (chosen[:, :, None] > 0) & (
        rank[:, :, None] == jnp.arange(cap, dtype=jnp.int32)[None, None, :]
    )
    weights = jnp.where(place, gates[:, :, None], 0.0).reshape(tok, slots)
    place = place.astype(BF16).reshape(tok, slots)
    send = lax.dot_general(place, h, (((0,), (0,)), ((), ())), preferred_element_type=F32).astype(
        BF16
    )
    got = lax.all_to_all(
        send.reshape(ep_count, cap, -1), "ep", split_axis=0, concat_axis=0, tiled=True
    )
    rows = lax.all_gather(got.reshape(slots, -1), "tp", axis=1, tiled=True)
    rows_f = rows.astype(F32)
    mean_sq = jnp.mean(rows_f * rows_f, axis=-1, keepdims=True)
    normed = (rows_f * lax.rsqrt(mean_sq + 1e-05) * norm_gain).astype(BF16)
    nt = (((1,), (1,)), ((), ()))
    gate_pre = lax.dot_general(w_gate[0], normed, nt, preferred_element_type=F32)
    up_pre = lax.dot_general(w_up[0], normed, nt, preferred_element_type=F32)
    act = (jax.nn.silu(gate_pre) * up_pre).astype(BF16)
    act_all = lax.all_gather(act, "tp", axis=0, tiled=True)
    out = lax.dot_general(
        act_all, down_cols, (((0,), (0,)), ((), ())), preferred_element_type=F32
    ).astype(BF16)
    back = lax.all_to_all(
        out.reshape(ep_count, cap, -1), "ep", split_axis=0, concat_axis=0, tiled=True
    )
    moe = jnp.dot(weights, back.reshape(slots, -1).astype(F32), precision=lax.Precision.HIGHEST)
    layer = (h.astype(F32) + moe).astype(BF16)
    return lax.all_to_all(layer, "tp", split_axis=0, concat_axis=1, tiled=True)


def solution(mesh):
    in_specs = (
        P("ep", "tp"),
        P(("ep", "tp"), None),
        P(),
        P("ep", None),
        P("ep", None),
        P("ep", "tp", None),
        P("ep", "tp", None),
        P("ep", "tp", None),
    )
    return jax.shard_map(
        per_device, mesh=mesh, in_specs=in_specs, out_specs=P(("ep", "tp"), None), check_vma=False
    )
```

profile of v0, /device:TPU:2, one launch (start us, length us, event | category | flops | bytes accessed | tf_op | source)
XLA Modules:
  0.0 219.9 jit_solution(954548781873976257)
XLA Ops:
  6.5 0.0 copy-start
  6.5 0.0 copy-start.6
  6.5 1.5 copy.37
  8.1 7.1 %all-to-all-start = ((bf16[16,8,256]{2,0,1:T(8,128)(2,1)}), bf16[16,8,256]{2,0,1:T(8,128)(2,1)S(1)}, u32[]{:S(2)}, u32[]{:S(2)}) async-start(bf16[16,8,256]{2,0,1:T(8,128)(2,1)} %bitcast.54), calls=%async_computation | async-start | bytes 131072 | tf_op jit(solution)/shard_map/all_to_all | solution.py:15
  15.2 0.0 all-gather.3.cloned.1.call-start
  15.2 0.7 fusion.19
  16.0 0.1 eq.45
  16.0 0.2 convolution_convert_fusion.2
  16.3 0.2 fusion.14
  16.5 7.1 %all-to-all-done = bf16[16,8,256]{2,0,1:T(8,128)(2,1)S(1)} async-done(((bf16[16,8,256]{2,0,1:T(8,128)(2,1)}), bf16[16,8,256]{2,0,1:T(8,128)(2,1)S(1)}, u32[]{:S(2)}, u32[]{:S(2)}) %all-to-all-start) | async-done | bytes 65568 | tf_op jit(solution)/shard_map/all_to_all | solution.py:15
  23.6 0.9 fusion.20
  24.4 0.3 convolution_convert_fusion.1
  24.7 31.3 %all_to_all.61 = bf16[64,16,256]{2,1,0:T(8,128)(2,1)} all-to-all(bf16[64,16,256]{2,1,0:T(8,128)(2,1)S(1)} %bitcast.57), channel_id=1, replica_groups=mesh['ep'=64,'tp'=8] {'ep'}, dimensions={0} | all-to-all | bytes 1048576 | tf_op jit(solution)/shard_map/all_to_all | solution.py:31
  56.0 0.0 all-gather.3.cloned.1.call-update
  56.1 0.0 all-gather.5.cloned.1.call-start
  56.1 56.3 %all-gather.3.cloned.1.call-done = bf16[1024,2048]{1,0:T(8,128)(2,1)} async-done(((bf16[1024,256]{1,0:T(8,128)(2,1)}), bf16[1024,2048]{1,0:T(8,128)(2,1)}) %all-gather.3.cloned.1.call-update) | async-done | bytes 4194320 | tf_op jit(solution)/shard_map/all_gather | solution.py:34
  112.4 0.0 copy-start.1
  112.4 3.2 %fusion = f32[1024]{0:T(1024)S(1)} fusion(bf16[1024,2048]{1,0:T(8,128)(2,1)} %all-gather.3.cloned.1.call-done), kind=kLoop, calls=%fused_computation.2 | loop fusion | flops 6290432 | bytes 4198400 | tf_op jit(solution)/shard_map/reduce_sum | solution.py:36
  115.6 0.0 copy-done
  115.7 0.0 copy-done.6
  115.7 0.2 copy-done.1
  115.9 0.0 copy-start.5
  115.9 1.7 convolution_bitcast_fusion.1
  117.5 0.0 copy-done.5
  117.5 0.0 copy-start.2
  117.5 2.6 %fusion.4 = bf16[176,1024]{1,0:T(8,128)(2,1)} fusion(bf16[1024,2048]{1,0:T(8,128)(2,1)S(1)} %copy-done.1, f32[2048]{0:T(1024)S(1)} %copy-done.6, f32[1024]{0:T(1024)S(1)} %add_rsqrt_fusion, bf16[1,176,2048]{2,1,0:T(8,128)(2,1)S(1)} %copy-done.5, f32[176,1024]{1,0:T(8,128)S(1)} %convolution_bitcast_fusion.1), kind=kOutput, calls=%fused_computation.10 | convolution fusion | flops 747667456 | bytes 6008832 | tf_op jit(solution)/shard_map/dot_general | solution.py:40
  120.1 0.0 all-gather.5.cloned.1.call-update
  120.1 0.0 copy-done.2
  120.1 0.2 copy.35
  120.3 0.1 copy.31
  120.5 0.0 copy-start.3
  120.5 0.0 copy-start.4
  120.5 23.5 %all_to_all.62 = bf16[176,8,256]{2,0,1:T(8,128)(2,1)S(1)} all-to-all(bf16[176,8,256]{2,0,1:T(8,128)(2,1)S(1)} %copy.31), channel_id=1, replica_groups=mesh['ep'=64,'tp'=8] {'tp'}, dimensions={1} | all-to-all | bytes 1441792 | tf_op jit(solution)/shard_map/all_to_all | solution.py:16
  144.0 23.3 %all-gather.5.cloned.1.call-done = bf16[1408,1024]{1,0:T(8,128)(2,1)} async-done(((bf16[176,1024]{1,0:T(8,128)(2,1)}), bf16[1408,1024]{1,0:T(8,128)(2,1)}) %all-gather.5.cloned.1.call-update) | async-done | bytes 2883600 | tf_op jit(solution)/shard_map/all_gather | solution.py:42
  167.3 3.6 %convolution_convert_fusion = bf16[1024,256]{1,0:T(8,128)(2,1)} fusion(bf16[1408,1024]{1,0:T(8,128)(2,1)} %all-gather.5.cloned.1.call-done, bf16[1408,256]{1,0:T(8,128)(2,1)S(1)} %bitcast.59), kind=kOutput, calls=%fused_computation.5 | convolution fusion | flops 738459648 | bytes 4128768 | tf_op jit(solution)/shard_map/dot_general | solution.py:43
  170.9 10.9 %all-to-all-start.3 = ((bf16[64,16,256]{2,1,0:T(8,128)(2,1)}), bf16[64,16,256]{2,1,0:T(8,128)(2,1)S(1)}, u32[]{:S(2)}, u32[]{:S(2)}) async-start(bf16[64,16,256]{2,1,0:T(8,128)(2,1)} %bitcast.12), calls=%async_computation.3 | async-start | bytes 1048576 | tf_op jit(solution)/shard_map/all_to_all | solution.py:46
  181.8 0.0 copy-done.3
  181.8 0.0 copy-done.4
  181.9 17.5 %all-to-all-done.3 = bf16[64,16,256]{2,1,0:T(8,128)(2,1)S(1)} async-done(((bf16[64,16,256]{2,1,0:T(8,128)(2,1)}), bf16[64,16,256]{2,1,0:T(8,128)(2,1)S(1)}, u32[]{:S(2)}, u32[]{:S(2)}) %all-to-all-start.3) | async-done | bytes 524320 | tf_op jit(solution)/shard_map/all_to_all | solution.py:46
  199.4 0.6 fusion.8
  200.0 12.5 %all_to_all.63 = bf16[8,16,256]{2,1,0:T(8,128)(2,1)S(1)} all-to-all(bf16[8,16,256]{2,1,0:T(8,128)(2,1)S(1)} %bitcast.62), channel_id=1, replica_groups=mesh['ep'=64,'tp'=8] {'tp'}, dimensions={0} | all-to-all | bytes 131072 | tf_op jit(solution)/shard_map/all_to_all | solution.py:51
  212.5 0.6 copy.34
  (5 shorter events, 0.1 us)
Async XLA Ops:
  6.5 109.1 %copy-start = (bf16[1,176,2048]{2,1,0:T(8,128)(2,1)S(1)}, bf16[1,176,2048]{2,1,0:T(8,128)(2,1)}, u32[]{:S(2)}) copy-start(bf16[1,176,2048]{2,1,0:T(8,128)(2,1)} %param.13) | copy-start | bytes 2162692
  6.5 109.1 %copy-start.6 = (f32[2048]{0:T(1024)S(1)}, f32[2048]{0:T(1024)}, u32[]{:S(2)}) copy-start(f32[2048]{0:T(1024)} %param.10) | copy-start | bytes 24580
  8.1 15.5 %all-to-all-start = ((bf16[16,8,256]{2,0,1:T(8,128)(2,1)}), bf16[16,8,256]{2,0,1:T(8,128)(2,1)S(1)}, u32[]{:S(2)}, u32[]{:S(2)}) async-start(bf16[16,8,256]{2,0,1:T(8,128)(2,1)} %bitcast.54), calls=%async_computation | async-start | bytes 131072 | tf_op jit(solution)/shard_map/all_to_all | solution.py:15
  15.2 97.2 %all-gather.3.cloned.1.call-start = ((), (), s32[]{:S(2)}) async-start(), calls=%async_computation.5 | async-start | bytes 4718592 | tf_op jit(solution)/shard_map/all_gather | solution.py:34
  56.1 111.2 %all-gather.5.cloned.1.call-start = ((), (), s32[]{:S(2)}) async-start(), calls=%async_computation.6 | async-start | bytes 3244032 | tf_op jit(solution)/shard_map/all_gather | solution.py:42
  112.4 3.4 %copy-start.1 = (bf16[1024,2048]{1,0:T(8,128)(2,1)S(1)}, bf16[1024,2048]{1,0:T(8,128)(2,1)}, u32[]{:S(2)}) copy-start(bf16[1024,2048]{1,0:T(8,128)(2,1)} %all-gather.3.cloned.1.call-done) | copy-start | bytes 12582916
  115.9 1.7 copy-start.5
  117.5 2.6 %copy-start.2 = (bf16[1,176,2048]{2,1,0:T(8,128)(2,1)S(1)}, bf16[1,176,2048]{2,1,0:T(8,128)(2,1)}, u32[]{:S(2)}) copy-start(bf16[1,176,2048]{2,1,0:T(8,128)(2,1)} %param.15) | copy-start | bytes 2162692
  120.5 61.3 %copy-start.3 = (s32[128,6]{0,1:T(8,128)S(1)}, s32[128,6]{0,1:T(8,128)}, u32[]{:S(2)}) copy-start(s32[128,6]{0,1:T(8,128)} %param.11) | copy-start | bytes 9220
  120.5 61.3 %copy-start.4 = (f32[128,6]{0,1:T(8,128)S(1)}, f32[128,6]{0,1:T(8,128)}, u32[]{:S(2)}) copy-start(f32[128,6]{0,1:T(8,128)} %param.12) | copy-start | bytes 9220
  170.9 28.4 %all-to-all-start.3 = ((bf16[64,16,256]{2,1,0:T(8,128)(2,1)}), bf16[64,16,256]{2,1,0:T(8,128)(2,1)S(1)}, u32[]{:S(2)}, u32[]{:S(2)}) async-start(bf16[64,16,256]{2,1,0:T(8,128)(2,1)} %bitcast.12), calls=%async_computation.3 | async-start | bytes 1048576 | tf_op jit(solution)/shard_map/all_to_all | solution.py:46
Sparse Core Ops, SparseCore 0:
  56.2 56.1 all-gather.2
  120.3 46.9 all-gather.4
where the time goes:
time: 220 us
  waiting for transfers between devices  104 us (47%)
  blocking collectives  67.3 us (31%)
  starting transfers between devices  18.1 us (8%)
  between operations  13.6 us (6%)
  matrix products  8.98 us (4%)
  other arithmetic  5.07 us (2%)
  local copies, waits for them, and re-layouts  2.79 us (1%)
    all_gather x1, waiting for transfers between devices, per_device(): rows = lax.all_gather(got.reshape(slots, -1), 'tp', axis=1, tiled=True)  56.3 us
    all_to_all x1, blocking collectives, per_device(): lax.all_to_all(send.reshape(ep_count, cap, -1), 'ep', split_axis=0, conca...  31.3 us
    all_to_all x1, blocking collectives, per_device(): lax.all_to_all(w_down[0], 'tp', split_axis=1, concat_axis=0, tiled=True)  23.5 us
    all_gather x1, waiting for transfers between devices, per_device(): act_all = lax.all_gather(act, 'tp', axis=0, tiled=True)  23.3 us
    all_to_all x1, waiting for transfers between devices, per_device(): lax.all_to_all(out.reshape(ep_count, cap, -1), 'ep', split_axis=0, concat...  17.5 us
    all_to_all x1, blocking collectives, per_device(): return lax.all_to_all(layer, 'tp', split_axis=0, concat_axis=1, tiled=True)  12.5 us
    all_to_all x1, starting transfers between devices, per_device(): lax.all_to_all(out.reshape(ep_count, cap, -1), 'ep', split_axis=0, concat...  10.9 us
    all_to_all x1, starting transfers between devices, per_device(): lax.all_to_all(resid, 'tp', split_axis=1, concat_axis=0, tiled=True)  7.1 us
  transfers between devices with their start and end apart: 4, of which 4 were waited for; matrix products, arithmetic and copies ran while one was open for 1% of the time, Pallas kernels for 0%

commit v1 on v0

--- a/solution.py
+++ b/solution.py
@@ -39,7 +39,15 @@
     gate_pre = lax.dot_general(w_gate[0], normed, nt, preferred_element_type=F32)
     up_pre = lax.dot_general(w_up[0], normed, nt, preferred_element_type=F32)
     act = (jax.nn.silu(gate_pre) * up_pre).astype(BF16)
-    act_all = lax.all_gather(act, "tp", axis=0, tiled=True)
+    act_all = jnp.concatenate(
+        lax.all_to_all(
+            jnp.stack([act] * lax.psum(1, axis_name="tp")),
+            axis_name="tp",
+            split_axis=0,
+            concat_axis=0,
+        ),
+        axis=0,
+    )
     out = lax.dot_general(
         act_all, down_cols, (((0,), (0,)), ((), ())), preferred_element_type=F32
     ).astype(BF16)

time: 220 us -> 251 us (1.14)
  blocking collectives: 67.3 us -> 110 us
  waiting for transfers between devices: 104 us -> 90 us
  starting transfers between devices: 18.1 us -> 21.1 us
  matrix products: 8.98 us -> 6.29 us
    all_to_all x1, blocking collectives: 23.5 us -> 67.5 us  [per_device(): lax.all_to_all(jnp.stack([act] * lax.psum(1, axis_name='tp')), axis_name=...]
    all_gather x1 -> x0, waiting for transfers between devices: 23.3 us -> none  [per_device(): act_all = lax.all_gather(act, 'tp', axis=0, tiled=True)]
    all_gather x1, waiting for transfers between devices: 56.3 us -> 65.5 us  [per_device(): rows = lax.all_gather(got.reshape(slots, -1), 'tp', axis=1, tiled=True)]
    all_to_all x0 -> x1, starting transfers between devices: none -> 3.54 us  [per_device(): lax.all_to_all(w_down[0], 'tp', split_axis=1, concat_axis=0, tiled=True)]
  transfers between devices with their start and end apart: 4 -> 4, of which waited for: 4 -> 3; matrix products, arithmetic and copies ran while one was open for 1% -> 4% of each run, Pallas kernels for 0% -> 0%
where the time goes in v1:
time: 251 us
  blocking collectives  110 us (44%)
  waiting for transfers between devices  90 us (36%)
  starting transfers between devices  21.1 us (8%)
  between operations  13.6 us (5%)
  matrix products  6.29 us (3%)
  local copies, waits for them, and re-layouts  5.12 us (2%)
  other arithmetic  5.07 us (2%)
    all_to_all x1, blocking collectives, per_device(): lax.all_to_all(jnp.stack([act] * lax.psum(1, axis_name='tp')), axis_name=...  67.5 us
    all_gather x1, waiting for transfers between devices, per_device(): rows = lax.all_gather(got.reshape(slots, -1), 'tp', axis=1, tiled=True)  65.5 us
    all_to_all x1, blocking collectives, per_device(): lax.all_to_all(send.reshape(ep_count, cap, -1), 'ep', split_axis=0, conca...  31.3 us
    all_to_all x1, waiting for transfers between devices, per_device(): lax.all_to_all(out.reshape(ep_count, cap, -1), 'ep', split_axis=0, concat...  17.5 us
    all_to_all x1, blocking collectives, per_device(): return lax.all_to_all(layer, 'tp', split_axis=0, concat_axis=1, tiled=True)  10.8 us
    all_to_all x1, starting transfers between devices, per_device(): lax.all_to_all(out.reshape(ep_count, cap, -1), 'ep', split_axis=0, concat...  10.4 us
    all_to_all x1, starting transfers between devices, per_device(): lax.all_to_all(resid, 'tp', split_axis=1, concat_axis=0, tiled=True)  7.1 us
    all_to_all x1, waiting for transfers between devices, per_device(): lax.all_to_all(resid, 'tp', split_axis=1, concat_axis=0, tiled=True)  7.07 us
  transfers between devices with their start and end apart: 4, of which 3 were waited for; matrix products, arithmetic and copies ran while one was open for 4% of the time, Pallas kernels for 0%

profile of v1, /device:TPU:2, one launch (start us, length us, event | category | flops | bytes accessed | tf_op | source)
XLA Modules:
  0.0 250.7 jit_solution(17047149415699948302)
XLA Ops:
  6.5 0.0 copy-start
  6.5 1.5 copy.33
  8.1 7.1 %all-to-all-start = ((bf16[16,8,256]{2,0,1:T(8,128)(2,1)}), bf16[16,8,256]{2,0,1:T(8,128)(2,1)S(1)}, u32[]{:S(2)}, u32[]{:S(2)}) async-start(bf16[16,8,256]{2,0,1:T(8,128)(2,1)} %bitcast.57), calls=%async_computation | async-start | bytes 131072 | tf_op jit(solution)/shard_map/all_to_all | solution.py:15
  15.2 0.0 all-gather.2.cloned.1.call-start
  15.2 0.7 fusion.21
  16.0 0.1 eq.45
  16.0 0.2 convolution_convert_fusion.1
  16.3 0.2 fusion.16
  16.5 7.1 %all-to-all-done = bf16[16,8,256]{2,0,1:T(8,128)(2,1)S(1)} async-done(((bf16[16,8,256]{2,0,1:T(8,128)(2,1)}), bf16[16,8,256]{2,0,1:T(8,128)(2,1)S(1)}, u32[]{:S(2)}, u32[]{:S(2)}) %all-to-all-start) | async-done | bytes 65568 | tf_op jit(solution)/shard_map/all_to_all | solution.py:15
  23.6 0.9 fusion.22
  24.4 0.3 convolution_convert_fusion
  24.7 31.3 %all_to_all.63 = bf16[64,16,256]{2,1,0:T(8,128)(2,1)} all-to-all(bf16[64,16,256]{2,1,0:T(8,128)(2,1)S(1)} %bitcast.60), channel_id=1, replica_groups=mesh['ep'=64,'tp'=8] {'ep'}, dimensions={0} | all-to-all | bytes 1048576 | tf_op jit(solution)/shard_map/all_to_all | solution.py:31
  56.0 0.0 all-gather.2.cloned.1.call-update
  56.0 0.0 copy-start.5
  56.1 1.3 copy.31
  57.4 1.0 copy.27
  58.4 3.5 %all-to-all-start.3 = ((bf16[176,8,256]{2,0,1:T(8,128)(2,1)}), bf16[176,8,256]{2,0,1:T(8,128)(2,1)S(1)}, u32[]{:S(2)}, u32[]{:S(2)}) async-start(bf16[176,8,256]{2,0,1:T(8,128)(2,1)} %copy.27), calls=%async_computation.3 | async-start | bytes 1441792 | tf_op jit(solution)/shard_map/all_to_all | solution.py:16
  61.9 65.5 %all-gather.2.cloned.1.call-done = bf16[1024,2048]{1,0:T(8,128)(2,1)} async-done(((bf16[1024,256]{1,0:T(8,128)(2,1)}), bf16[1024,2048]{1,0:T(8,128)(2,1)}) %all-gather.2.cloned.1.call-update) | async-done | bytes 4194320 | tf_op jit(solution)/shard_map/all_gather | solution.py:34
  127.4 0.0 copy-start.1
  127.4 3.2 %fusion = f32[1024]{0:T(1024)S(1)} fusion(bf16[1024,2048]{1,0:T(8,128)(2,1)} %all-gather.2.cloned.1.call-done), kind=kLoop, calls=%fused_computation.2 | loop fusion | flops 6290432 | bytes 4198400 | tf_op jit(solution)/shard_map/reduce_sum | solution.py:36
  130.6 0.0 copy-done
  130.6 0.0 copy-done.5
  130.6 0.2 copy-done.1
  130.8 0.0 copy-start.4
  130.8 1.6 convolution_bitcast_fusion.2
  132.4 0.0 copy-done.4
  132.5 1.7 fusion.5
  134.2 0.0 all-to-all-done.3
  134.2 0.4 stack.2
  134.6 67.5 %all_to_all.64 = bf16[8,176,1024]{2,1,0:T(8,128)(2,1)S(1)} all-to-all(bf16[8,176,1024]{2,1,0:T(8,128)(2,1)S(1)} %stack.2), channel_id=1, replica_groups=mesh['ep'=64,'tp'=8] {'tp'}, dimensions={0} | all-to-all | bytes 5767168 | tf_op jit(solution)/shard_map/all_to_all | solution.py:43
  202.1 0.0 copy-start.2
  202.1 0.0 copy-start.3
  202.1 1.8 fusion.3
  203.9 10.4 %all-to-all-start.4 = ((bf16[64,16,256]{2,1,0:T(8,128)(2,1)}), bf16[64,16,256]{2,1,0:T(8,128)(2,1)S(1)}, u32[]{:S(2)}, u32[]{:S(2)}) async-start(bf16[64,16,256]{2,1,0:T(8,128)(2,1)} %bitcast.12), calls=%async_computation.4 | async-start | bytes 1048576 | tf_op jit(solution)/shard_map/all_to_all | solution.py:54
  214.3 0.0 copy-done.2
  214.3 0.0 copy-done.3
  214.4 17.5 %all-to-all-done.4 = bf16[64,16,256]{2,1,0:T(8,128)(2,1)S(1)} async-done(((bf16[64,16,256]{2,1,0:T(8,128)(2,1)}), bf16[64,16,256]{2,1,0:T(8,128)(2,1)S(1)}, u32[]{:S(2)}, u32[]{:S(2)}) %all-to-all-start.4) | async-done | bytes 524320 | tf_op jit(solution)/shard_map/all_to_all | solution.py:54
  231.8 0.6 fusion.9
  232.4 10.8 %all_to_all.65 = bf16[8,16,256]{2,1,0:T(8,128)(2,1)S(1)} all-to-all(bf16[8,16,256]{2,1,0:T(8,128)(2,1)S(1)} %bitcast.64), channel_id=1, replica_groups=mesh['ep'=64,'tp'=8] {'tp'}, dimensions={0} | all-to-all | bytes 131072 | tf_op jit(solution)/shard_map/all_to_all | solution.py:59
  243.2 0.6 copy.30
  (5 shorter events, 0.1 us)
Async XLA Ops:
  6.5 124.1 %copy-start = (bf16[1,176,2048]{2,1,0:T(8,128)(2,1)S(1)}, bf16[1,176,2048]{2,1,0:T(8,128)(2,1)}, u32[]{:S(2)}) copy-start(bf16[1,176,2048]{2,1,0:T(8,128)(2,1)} %param.13) | copy-start | bytes 2162692
  8.1 15.5 %all-to-all-start = ((bf16[16,8,256]{2,0,1:T(8,128)(2,1)}), bf16[16,8,256]{2,0,1:T(8,128)(2,1)S(1)}, u32[]{:S(2)}, u32[]{:S(2)}) async-start(bf16[16,8,256]{2,0,1:T(8,128)(2,1)} %bitcast.57), calls=%async_computation | async-start | bytes 131072 | tf_op jit(solution)/shard_map/all_to_all | solution.py:15
  15.2 112.2 %all-gather.2.cloned.1.call-start = ((), (), s32[]{:S(2)}) async-start(), calls=%async_computation.6 | async-start | bytes 4718592 | tf_op jit(solution)/shard_map/all_gather | solution.py:34
  56.0 74.6 %copy-start.5 = (f32[2048]{0:T(1024)S(1)}, f32[2048]{0:T(1024)}, u32[]{:S(2)}) copy-start(f32[2048]{0:T(1024)} %param.10) | copy-start | bytes 24580
  58.4 75.8 %all-to-all-start.3 = ((bf16[176,8,256]{2,0,1:T(8,128)(2,1)}), bf16[176,8,256]{2,0,1:T(8,128)(2,1)S(1)}, u32[]{:S(2)}, u32[]{:S(2)}) async-start(bf16[176,8,256]{2,0,1:T(8,128)(2,1)} %copy.27), calls=%async_computation.3 | async-start | bytes 1441792 | tf_op jit(solution)/shard_map/all_to_all | solution.py:16
  127.4 3.4 %copy-start.1 = (bf16[1024,2048]{1,0:T(8,128)(2,1)S(1)}, bf16[1024,2048]{1,0:T(8,128)(2,1)}, u32[]{:S(2)}) copy-start(bf16[1024,2048]{1,0:T(8,128)(2,1)} %all-gather.2.cloned.1.call-done) | copy-start | bytes 12582916
  130.8 1.6 copy-start.4
  202.1 12.2 %copy-start.2 = (s32[128,6]{0,1:T(8,128)S(1)}, s32[128,6]{0,1:T(8,128)}, u32[]{:S(2)}) copy-start(s32[128,6]{0,1:T(8,128)} %param.11) | copy-start | bytes 9220
  202.1 12.2 %copy-start.3 = (f32[128,6]{0,1:T(8,128)S(1)}, f32[128,6]{0,1:T(8,128)}, u32[]{:S(2)}) copy-start(f32[128,6]{0,1:T(8,128)} %param.12) | copy-start | bytes 9220
  203.9 27.9 %all-to-all-start.4 = ((bf16[64,16,256]{2,1,0:T(8,128)(2,1)}), bf16[64,16,256]{2,1,0:T(8,128)(2,1)S(1)}, u32[]{:S(2)}, u32[]{:S(2)}) async-start(bf16[64,16,256]{2,1,0:T(8,128)(2,1)} %bitcast.12), calls=%async_computation.4 | async-start | bytes 1048576 | tf_op jit(solution)/shard_map/all_to_all | solution.py:54
Sparse Core Ops, SparseCore 0:
  56.2 71.1 all-gather.1
